TPU v7x, 32 devices: a whole 2x2x4 slice. The times are simulated.
32 devices in a mesh: rows: 8 (over z, y), cols: 4 (over x, core).
Axes of the slice: x: 2, y: 2, z: 4, core: 2. Of those that a mesh axis runs over, the one named last changes fastest.
Arguments:
- depth: float32 [128, 16384], P('rows', 'cols'), may hold values from 0.08 to 6.3, as said below
- hit_mask: int32 [128, 16384], P('rows', 'cols'), may hold values 0 or 1
- hit_count: int32 [128, 16384], P('rows', 'cols'), may hold values from 1 to 8
- grad_h: float32 [128, 16384], P('rows', 'cols'), may hold values from -6 to 6
- grad_v: float32 [128, 16384], P('rows', 'cols'), may hold values from -6 to 6
Outputs:
- solution_field: float32 [128, 16384], P('rows', 'cols')
- residual: float32 [128, 16384], P('rows', 'cols')
Inputs may be any that keep to these rules, and one draw needn't show every extreme that they name: `depth`: positive depths.
All inputs are finite; a program needn't handle non-finite values. No bound on the sum of `hit_mask` on one device may be relied on, other than what follows from the above.
Results may differ from a plain program's by a relative error of at most 0.0003.
Values sent between devices are 32-bit elements; how exact they have to be, the bound alone decides.
A program may use at most 64 MiB of HBM per device.

v0:
```python
import functools

import jax
import jax.numpy as jnp
from jax import lax
from jax.experimental import pallas as pl
from jax.experimental.pallas import tpu as pltpu
from jax.sharding import PartitionSpec as P

ITERS = 12

prior_weight = 0.1
smooth_weight = 2.0
LANES = 128
SUB = 8
HALF = LANES // 2
MESH = pl.DeviceIdType.MESH

SCALE = 0.25
CENTER = 9.0 * SCALE
SPREAD = 16.0 * SCALE * SCALE
BLOCKS = (2, 2, 3, 3, 2)
KNOWN = 4
SWITCH = 7
DEPTH = max(BLOCKS)
GHOST = SUB
COPIES = 64


def each(start, stop, body):
    if stop - start < 32:
        for k in range(start, stop):
            body(k)
    else:
        lax.fori_loop(start, stop, lambda k, c: (body(k), c)[1], 0)


def factor(gram, size):
    s = {key: value for key, value in gram.items()}
    lower, pivots = {}, []
    for k in range(size):
        pivots.append(s[k, k])
        if k + 1 == size:
            break
        inverse = 1.0 / s[k, k]
        for i in range(k + 1, size):
            lower[i, k] = s[i, k] * inverse
        for i in range(k + 1, size):
            for j in range(k + 1, i + 1):
                if (i, j) in s:
                    s[i, j] = s[i, j] - lower[i, k] * s[j, k]
    return lower, pivots


def lanczos(gram, size, a):
    lower, pivots = factor(gram, size + 1)
    alphas = []
    for k in range(size):
        value = a[k] + lower[k + 1, k]
        alphas.append(value - lower[k, k - 1] if k else value)
    betas = [None] + [pivots[k] / pivots[k - 1] for k in range(1, len(pivots))]
    return alphas, betas


def added(x, y):
    return y if x is None else (x if y is None else x + y)


def times(c, x):
    return None if x is None or c is None else (x if isinstance(c, float) and c == 1.0 else c * x)


def minus(x, y):
    return x if y is None else (-y if x is None else x - y)


def applied(p, a, b, size):
    out = [None] * size
    for k, value in enumerate(p):
        if value is None:
            continue
        out[k] = added(out[k], times(a[k], value))
        if k + 1 < size:
            out[k + 1] = added(out[k + 1], value)
        if k:
            out[k - 1] = added(out[k - 1], times(b[k], value))
    return out


def kernel(
    nr, nc, rows, cols,
    depth, hit_mask, hit_count, grad_h, grad_v,
    x_out, r_out,
    basis, coef, strip, strip_coef, strip_next, strip_flow,
    edge_send, edge_left, edge_right, folds, by_device,
    send, recv, sum_send, sum_recv,
):
    me_r = lax.axis_index("rows")
    me_c = lax.axis_index("cols")
    J = cols // (SUB * LANES)
    tiles = cols // LANES
    R, D = rows, DEPTH
    bands = rows // SUB
    tall = rows + 2 * GHOST
    has_above, has_below = me_r > 0, me_r < nr - 1
    has_left, has_right = me_c > 0, me_c < nc - 1
    up, down = (me_r - 1, me_c), (me_r + 1, me_c)
    lefthand, righthand = (me_r, me_c - 1), (me_r, me_c + 1)
    devices = nr * nc
    me = me_r * nc + me_c

    def peer(k):
        other = lax.rem(me + k, devices)
        return (other // nc, lax.rem(other, nc))

    barrier = pltpu.get_barrier_semaphore()
    each(1, devices, lambda k: pl.semaphore_signal(barrier, inc=1, device_id=peer(k), device_id_type=MESH))

    sub_id = lax.broadcasted_iota(jnp.int32, (SUB, LANES), 0)
    lane_id = lax.broadcasted_iota(jnp.int32, (SUB, LANES), 1)
    zero = jnp.zeros((SUB, LANES), jnp.float32)

    used = [0]
    pending = []

    def copy(src, dst, to, sends, receives):
        k = used[0]
        used[0] += 1
        c = pltpu.make_async_remote_copy(
            src_ref=src, dst_ref=dst, send_sem=send.at[k], recv_sem=recv.at[k], device_id=to, device_id_type=MESH
        )
        pl.when(sends)(c.start)
        pending.append((c, sends))
        return c, receives

    def arrive(copies):
        for c, receives in copies:
            pl.when(receives)(c.wait_recv)

    def local(read, last_col, last_row):
        confidence = (read(hit_mask) * read(hit_count)).astype(jnp.float32) + prior_weight
        h, v = read(grad_h), read(grad_v)
        e = (SCALE * smooth_weight) * jnp.exp(-0.5 * h * h)
        s = (SCALE * smooth_weight) * jnp.exp(-0.5 * v * v)
        if last_col is not None:
            e = jnp.where(jnp.logical_and(last_col, jnp.logical_not(has_right)), 0.0, e)
        if last_row is not None:
            s = jnp.where(jnp.logical_and(last_row, jnp.logical_not(has_below)), 0.0, s)
        return SCALE * confidence, e, s, confidence * read(depth)

    for side in range(2):
        tile = (tiles - 1) * side
        for band in range(bands):
            start = (band * tiles + tile) * SUB
            values = local(
                lambda ref: ref[start : start + SUB, :],
                lane_id == LANES - 1 if side else None,
                sub_id == SUB - 1 if band == bands - 1 else None,
            )
            for n, value in enumerate(values):
                edge_send[side, band, n] = value

    def row_coefficients(r, last_row):
        band, within = r // SUB, lax.rem(r, SUB)
        for j in range(J):
            start = band * (tiles * SUB) + j * SUB + within
            c, e, s, b = local(
                lambda ref: ref[pl.ds(start, SUB, stride=J * SUB), :],
                jnp.logical_and(lane_id == LANES - 1, sub_id == SUB - 1) if j == J - 1 else None,
                sub_id >= 0 if last_row else None,
            )
            coef[0, D + r, j] = c
            coef[1, D + r, j] = e
            coef[2, D + r, j] = s
            basis[0, D + r, j] = b

    def coefficient_rows(start, stop, last=False):
        for r in range(start, stop):
            row_coefficients(r, last and r == R - 1)

    coefficient_rows(0, D)
    lax.fori_loop(0, (R - 2 * D) // 2, lambda i, c: ([row_coefficients(D + 2 * i + t, False) for t in range(2)], c)[1], 0)
    coefficient_rows(D + (R - 2 * D) // 2 * 2, R, True)

    def clear_ghost(first, strip_first):
        def _():
            for t in range(D):
                for j in range(J):
                    for n in range(3):
                        coef[n, first + t, j] = zero
                    for slot in exchanged:
                        basis[slot, first + t, j] = zero
            for side in range(2):
                for n in range(3):
                    strip_coef[n, side, strip_first : strip_first + GHOST, :] = zero
                for slot in strips_exchanged:
                    strip[slot, side, strip_first : strip_first + GHOST, :] = zero

        return _

    starts = [sum(BLOCKS[:n]) for n in range(len(BLOCKS))]

    def w_slot(k):
        return SWITCH + k if k else 0

    exchanged = sorted(
        {k if k < SWITCH else w_slot(k) for k in starts}
        | {(k - 1 if k < SWITCH else w_slot(k - 1)) for k in starts if k > 0}
        | set(range(SWITCH))
    )
    strips_exchanged = [0, w_slot(SWITCH - 1), w_slot(SWITCH)]
    pl.when(jnp.logical_not(has_above))(clear_ghost(0, 0))
    pl.when(jnp.logical_not(has_below))(clear_ghost(D + R, GHOST + R))

    @pl.when(jnp.logical_not(has_left))
    def _():
        edge_left[...] = jnp.zeros_like(edge_left)

    @pl.when(jnp.logical_not(has_right))
    def _():
        edge_right[...] = jnp.zeros_like(edge_right)

    pl.semaphore_wait(barrier, devices - 1)

    def send_rows(slot, first, count):
        if count <= 0:
            return []
        top = D + first - 1
        bottom = D + R - (first - 1) - count
        return [
            copy(basis.at[slot, pl.ds(top, count)], basis.at[slot, pl.ds(top + R, count)], up, has_above, has_below),
            copy(basis.at[slot, pl.ds(bottom, count)], basis.at[slot, pl.ds(bottom - R, count)], down, has_below, has_above),
        ]

    def send_coefs(old, new):
        copies = []
        count = new - old
        bottom = D + R - new
        copies.append(copy(coef.at[2, pl.ds(bottom, count)], coef.at[2, pl.ds(bottom - R, count)], down, has_below, has_above))
        low, high = max(old, 1), new - 1
        if high >= low:
            n = high - low + 1
            top = D + low - 1
            bottom = D + R - high
            copies.append(copy(coef.at[:, pl.ds(top, n)], coef.at[:, pl.ds(top + R, n)], up, has_above, has_below))
            copies.append(
                copy(coef.at[0:2, pl.ds(bottom, n)], coef.at[0:2, pl.ds(bottom - R, n)], down, has_below, has_above)
            )
        return copies

    def send_strips(slots):
        copies = []
        for slot in slots:
            copies.append(
                copy(
                    strip.at[slot, :, pl.ds(GHOST, GHOST)], strip.at[slot, :, pl.ds(GHOST + R, GHOST)],
                    up, has_above, has_below,
                )
            )
            copies.append(
                copy(strip.at[slot, :, pl.ds(R, GHOST)], strip.at[slot, :, pl.ds(0, GHOST)], down, has_below, has_above)
            )
        return copies

    def rolled(v, shift, axis):
        return pltpu.roll(v, shift % v.shape[axis], axis)

    def strip_ready(src):
        v = strip[src, 0]
        strip_flow[...] = rolled(strip_coef[1, 0] * (v - rolled(v, -1, 1)), 1, 1)
        strip_next[...] = rolled(strip[src, 1], -1, 1)

    def tall_wide(c):
        return c if isinstance(c, float) else jnp.concatenate([c] * (tall // SUB), axis=0)

    def strip_step(src, prev, dst, a, b):
        for side in range(2):
            v = strip[src, side]
            flow = strip_coef[1, side] * (v - rolled(v, -1, 1))
            fall = strip_coef[2, side] * (v - rolled(v, -1, 0))
            value = (strip_coef[0, side] - tall_wide(a)) * v + (flow - rolled(flow, 1, 1)) + (fall - rolled(fall, 1, 0))
            if b is not None:
                value = value - times(tall_wide(b), strip[prev, side])
            strip[dst, side] = value

    def step(src, prev, dst, a, b, reach):
        first, count = D - reach, R + 2 * reach
        unroll = next(u for u in (5, 6, 4, 3, 2, 1) if count % u == 0)

        def row(i, state):
            v, fall_above = state
            below = [basis[src, i + 1, j] for j in range(J)]
            fall = [coef[2, i, j] * (v[j] - below[j]) for j in range(J)]
            line = pl.ds(i + (GHOST - D), 1)
            to_left = [rolled(v[j], -1, 1) for j in range(J)]
            beyond = jnp.where(
                sub_id == SUB - 1, jnp.broadcast_to(strip_next[line, :], (SUB, LANES)), rolled(to_left[0], -1, 0)
            )
            flow = [
                coef[1, i, j] * (v[j] - jnp.where(lane_id == LANES - 1, to_left[j + 1] if j + 1 < J else beyond, to_left[j]))
                for j in range(J)
            ]
            to_right = [rolled(f, 1, 1) for f in flow]
            before = jnp.where(
                sub_id == 0, jnp.broadcast_to(strip_flow[line, :], (SUB, LANES)), rolled(to_right[J - 1], 1, 0)
            )
            for j in range(J):
                arriving = jnp.where(lane_id == 0, to_right[j - 1] if j else before, to_right[j])
                value = (coef[0, i, j] - a) * v[j] + ((flow[j] - arriving) + (fall[j] - fall_above[j]))
                if b is not None:
                    value = value - times(b, basis[prev, i, j])
                basis[dst, i, j] = value
            return below, fall

        def body(n, state):
            for t in range(unroll):
                state = row(first + n * unroll + t, state)
            return state

        v = [basis[src, first, j] for j in range(J)]
        fall = [coef[2, first - 1, j] * (basis[src, first - 1, j] - v[j]) for j in range(J)]
        lax.fori_loop(0, count // unroll, body, (v, fall))

    def advance(src, prev, dst, a, b, reach, more=True):
        strip_ready(src)
        step(src, prev, dst, a, b, reach)
        if more:
            strip_step(src, prev, dst, a, b)

    def dots(pairs, base):
        for g in range(0, len(pairs), 8):
            group = pairs[g : g + 8]
            slots = sorted({s for pair in group for s in pair})

            def body(i, sums):
                for j in range(J):
                    held = {s: basis[s, D + i, j] for s in slots}
                    sums = tuple(total + held[p] * held[q] for total, (p, q) in zip(sums, group))
                return sums

            sums = lax.fori_loop(0, R, body, (zero,) * len(group), unroll=2)
            for n, total in enumerate(sums):
                k = base + g + n
                folds[k : k + 1, :] = jnp.sum(total, axis=0, keepdims=True)

    def combine(targets, first, count):
        slots = sorted({s for _, terms in targets for s in terms})

        def body(i, c):
            for j in range(J):
                held = {s: basis[s, first + i, j] for s in slots}
                for target, terms in targets:
                    total = None
                    for s, weight in terms.items():
                        total = added(total, times(weight, held[s]))
                    if callable(target):
                        target(i, j, total)
                    else:
                        basis[target, first + i, j] = total
            return c

        lax.fori_loop(0, count, body, 0)

    def reduce(slot, count):
        n = -(-count // SUB) * SUB
        part = jnp.broadcast_to(jnp.sum(folds[0:n, :], axis=1, keepdims=True), (n, LANES))
        mine = lax.broadcasted_iota(jnp.int32, (n, LANES), 0) == lax.broadcasted_iota(jnp.int32, (n, LANES), 1)
        by_device[slot, me] = jnp.sum(jnp.where(mine, part, 0.0), axis=0, keepdims=True)

        def outgoing(k):
            here = by_device.at[slot, me]
            return pltpu.make_async_remote_copy(
                src_ref=here, dst_ref=here, send_sem=sum_send.at[slot, k], recv_sem=sum_recv.at[slot, me],
                device_id=peer(k), device_id_type=MESH,
            )

        each(1, devices, lambda k: outgoing(k).start())

        def finish():
            def arrival(k):
                source = lax.rem(me + k, devices)
                here = by_device.at[slot, source]
                pltpu.make_async_remote_copy(
                    src_ref=here, dst_ref=here, send_sem=sum_send.at[slot, k], recv_sem=sum_recv.at[slot, source],
                    device_id=peer(k), device_id_type=MESH,
                ).wait_recv()

            each(1, devices, arrival)
            each(1, devices, lambda k: outgoing(k).wait_send())
            if devices <= 32:
                parts = [by_device[slot, k] for k in range(devices)]
                while len(parts) > 1:
                    parts = [a + b for a, b in zip(parts[::2], parts[1::2])] + parts[len(parts) // 2 * 2 :]
                total = parts[0]
            else:
                total = lax.fori_loop(1, devices, lambda k, t: t + by_device[slot, k], by_device[slot, 0])
            return [jnp.broadcast_to(total[:, k : k + 1], (SUB, LANES)) for k in range(count)]

        return finish

    v_a = [CENTER] * SWITCH
    v_b = [None, 2.0 * SPREAD] + [SPREAD] * (SWITCH - 1)

    opening = send_rows(0, 1, BLOCKS[0]) + send_coefs(0, BLOCKS[0])
    sides = [
        copy(edge_send.at[0], edge_right, lefthand, has_left, has_right),
        copy(edge_send.at[1], edge_left, righthand, has_right, has_left),
    ]
    arrive(sides)
    for band in range(bands):
        own = slice(GHOST + band * SUB, GHOST + (band + 1) * SUB)
        for n in range(4):
            here = strip_coef.at[n] if n < 3 else strip.at[0]
            here[0, own, :] = jnp.where(lane_id < HALF, edge_send[0, band, n], edge_left[band, n])
            here[1, own, :] = jnp.where(lane_id < HALF, edge_right[band, n], edge_send[1, band, n])
    ghosts = send_strips([0]) + [
        copy(strip_coef.at[:, :, pl.ds(GHOST, GHOST)], strip_coef.at[:, :, pl.ds(GHOST + R, GHOST)], up, has_above, has_below),
        copy(strip_coef.at[:, :, pl.ds(R, GHOST)], strip_coef.at[:, :, pl.ds(0, GHOST)], down, has_below, has_above),
    ]
    deeper = []
    finish = None
    k = 0
    w_a = w_b = None
    for n, block in enumerate(BLOCKS):
        slot = (lambda i: i) if k < SWITCH else w_slot
        if n == 0:
            arrive(opening + ghosts)
        else:
            first = send_rows(slot(k), 1, block) + send_rows(slot(k - 1), 2, block - 2)
            if k == SWITCH:
                first = first + send_strips([slot(k - 1), slot(k)])
            if n == 1 and BLOCKS[0] < D:
                deeper = send_coefs(BLOCKS[0], D)
            if k == KNOWN:
                pairs = [(i, j) for i in range(KNOWN + 1) for j in range(i + 1)]
                dots(pairs, 0)
                finish = reduce(0, len(pairs))
            if k == SWITCH:
                combine([(w_slot(i), {s: weights[i][s] for s in range(i + 1)}) for i in range(1, SWITCH - 1)], D, R)
                grams = [(i, j) for i in range(SWITCH + 1) for j in range(i + 1)]
                dots([(w_slot(i), w_slot(j)) for i, j in grams], 0)
            elif k > SWITCH:
                more = [(i, j) for i in range(starts[n - 1] + 1, k + 1) for j in range(i + 1)]
                dots([(w_slot(i), w_slot(j)) for i, j in more], len(grams))
                grams = grams + more
            arrive(first)
            if block == D and deeper:
                arrive(deeper)
                deeper = []
        for t in range(block):
            a = v_a[k] if k < SWITCH else w_a[k]
            b = v_b[k] if k < SWITCH else w_b[k]
            advance(slot(k), slot(k - 1) if k else None, slot(k + 1), a, b, block - 1 - t, k + 1 < ITERS)
            k += 1
        if k == SWITCH:
            totals = finish()
            gram = {pair: total for pair, total in zip(pairs, totals)}
            alphas, betas = lanczos(gram, KNOWN, v_a)
            w_a = alphas + [alphas[-1]] * (ITERS - KNOWN)
            w_b = betas + [betas[-1]] * (ITERS - KNOWN)
            one = jnp.ones((SUB, LANES), jnp.float32)
            weights = [[one]]
            for i in range(SWITCH):
                value = applied(weights[i] + [None], v_a + [None], v_b + [None], i + 2)
                value = [minus(p, times(w_a[i], q)) for p, q in zip(value, weights[i] + [None])]
                if i:
                    value = [minus(p, times(w_b[i], q)) for p, q in zip(value, weights[i - 1] + [None] * 2)]
                weights.append(value)
            final = [(w_slot(i), {s: weights[i][s] for s in range(i + 1)}) for i in (SWITCH - 1, SWITCH)]
            combine(final, D, R)
            combine(final[:1], D - 1, 1)
            combine(final[:1], D + R, 1)
            for target, terms in final:
                for side in range(2):
                    for band in range(bands):
                        own = slice(GHOST + band * SUB, GHOST + (band + 1) * SUB)
                        total = None
                        for s, weight in terms.items():
                            total = added(total, times(weight, strip[s, side, own, :]))
                        strip[target, side, own, :] = total

    more = [(i, j) for i in range(starts[-1] + 1, ITERS + 1) for j in range(i + 1) if j < ITERS]
    dots([(w_slot(i), w_slot(j)) for i, j in more], len(grams))
    grams = grams + more
    totals = reduce(1, len(grams))()
    gram = {pair: total for pair, total in zip(grams, totals)}
    gram[ITERS, ITERS] = zero
    alphas, betas = lanczos(gram, ITERS, w_a)
    one = jnp.ones((SUB, LANES), jnp.float32)
    x, r, p = [None] * (ITERS + 1), [one], [one]
    w_a = w_a + [None]
    w_b = w_b + [None]
    inverse = None
    for i in range(ITERS):
        pivot = alphas[i] if i == 0 else alphas[i] - betas[i] * inverse
        inverse = 1.0 / pivot
        image = applied(p + [None], w_a, w_b, i + 2)
        gain = SCALE * inverse
        x = [added(q, times(gain, s)) for q, s in zip(x, p + [None] * (ITERS + 1 - len(p)))]
        r = [minus(q, times(inverse, s)) for q, s in zip(r + [None], image)]
        if i + 1 < ITERS:
            ratio = betas[i + 1] * inverse * inverse
            p = [added(q, times(ratio, s)) for q, s in zip(r, p + [None])]

    def store(ref):
        def put(i, j, value):
            band, within = i // SUB, lax.rem(i, SUB)
            ref[pl.ds(band * (tiles * SUB) + j * SUB + within, SUB, stride=J * SUB), :] = value

        return put

    combine(
        [
            (store(x_out), {w_slot(i): x[i] for i in range(ITERS)}),
            (store(r_out), {w_slot(i): r[i] for i in range(ITERS + 1)}),
        ],
        D, R,
    )
    for c, sends in pending:
        pl.when(sends)(c.wait_send)


def solution(mesh):
    nr, nc = mesh.shape["rows"], mesh.shape["cols"]

    def on_device(*inputs):
        rows, cols = inputs[0].shape
        bands, tiles, chunk = rows // SUB, cols // LANES, cols // (SUB * LANES)

        def pieces(a):
            return a.reshape(bands, SUB, tiles, LANES).transpose(0, 2, 1, 3).reshape(bands * tiles * SUB, LANES)

        def whole(a):
            return a.reshape(bands, tiles, SUB, LANES).transpose(0, 2, 1, 3).reshape(rows, cols)

        def held(*shape):
            return pltpu.VMEM(shape, jnp.float32)

        block = jax.ShapeDtypeStruct((bands * tiles * SUB, LANES), jnp.float32)
        high, tall = rows + 2 * DEPTH, rows + 2 * GHOST
        slots = SWITCH + ITERS + 1
        dma = pltpu.SemaphoreType.DMA
        x, r = pl.pallas_call(
            functools.partial(kernel, nr, nc, rows, cols),
            out_shape=(block, block),
            in_specs=[pl.BlockSpec(memory_space=pltpu.VMEM)] * 5,
            out_specs=[pl.BlockSpec(memory_space=pltpu.VMEM)] * 2,
            scratch_shapes=[
                held(slots, high, chunk, SUB, LANES),
                held(3, high, chunk, SUB, LANES),
                held(slots, 2, tall, LANES),
                held(3, 2, tall, LANES),
                held(tall, LANES),
                held(tall, LANES),
                held(2, bands, 4, SUB, LANES),
                held(bands, 4, SUB, LANES),
                held(bands, 4, SUB, LANES),
                held(96, LANES),
                held(2, nr * nc, 1, LANES),
                dma((COPIES,)), dma((COPIES,)), dma((2, nr * nc)), dma((2, nr * nc)),
            ],
            compiler_params=pltpu.CompilerParams(collective_id=0, has_side_effects=True),
        )(*(pieces(a) for a in inputs))
        return whole(x), whole(r)

    spec = P("rows", "cols")
    return jax.shard_map(
        on_device, mesh=mesh, in_specs=(spec,) * 5, out_specs=(spec, spec), check_vma=False
    )
```

profile of v0, /device:TPU:0, one launch (start us, length us, event | category | flops | bytes accessed | tf_op | source)
XLA Modules:
  0.0 54.0 jit_solution(16134351252412745589)
XLA Ops:
  0.6 50.9 %shard_map.68 = (f32[512,128]{1,0:T(8,128)}, f32[512,128]{1,0:T(8,128)}) custom-call(f32[512,128]{1,0:T(8,128)} %bitcast.35, s32[512,128]{1,0:T(8,128)} %bitcast.36, s32[512,128]{1,0:T(8,128)} %bitcast.37, f32[512,128]{1,0:T(8,128)} %bitcast.38, f32[512,128]{1,0:T(8,128)} %bitcast.39), custom_call_target="tpu_custom_call" | custom-call | tf_op jit(solution)/shard_map/pallas_call | solution.py:543
  51.6 0.0 copy-start
  51.6 1.7 %copy.9 = f32[16,4096]{1,0:T(8,128)} copy(f32[16,4096]{1,0:T(8,128)} %bitcast.41) | data formatting | bytes 524288
  53.3 0.0 copy-done
  53.3 0.7 %copy.10 = f32[16,4096]{1,0:T(8,128)} copy(f32[16,4096]{1,0:T(8,128)S(1)} %bitcast.40) | data formatting | bytes 524288
Async XLA Ops:
  51.6 1.7 %copy-start = (f32[512,128]{1,0:T(8,128)S(1)}, f32[512,128]{1,0:T(8,128)}, u32[]{:S(2)}) copy-start(f32[512,128]{1,0:T(8,128)} %get-tuple-element.5) | copy-start | bytes 786436
where the time goes:
time: 54.1 us; the launch traced here: 54 us
  Pallas kernels  50.9 us (94%)
  local copies, waits for them, and re-layouts  2.42 us (4%)
  between operations  0.65 us (1%)
    pallas_call x1, Pallas kernels, on_device(): pl.pallas_call(functools.partial(kernel, nr, nc, rows, cols), out_shape=(...  50.9 us
    unnamed x4, local copies, waits for them, and re-layouts  2.42 us

commit v1 on v0

--- a/solution.py
+++ b/solution.py
@@ -35,31 +35,31 @@
         lax.fori_loop(start, stop, lambda k, c: (body(k), c)[1], 0)
 
 
-def factor(gram, size):
-    s = {key: value for key, value in gram.items()}
-    lower, pivots = {}, []
-    for k in range(size):
-        pivots.append(s[k, k])
-        if k + 1 == size:
-            break
-        inverse = 1.0 / s[k, k]
-        for i in range(k + 1, size):
-            lower[i, k] = s[i, k] * inverse
-        for i in range(k + 1, size):
-            for j in range(k + 1, i + 1):
-                if (i, j) in s:
-                    s[i, j] = s[i, j] - lower[i, k] * s[j, k]
-    return lower, pivots
-
-
-def lanczos(gram, size, a):
-    lower, pivots = factor(gram, size + 1)
-    alphas = []
-    for k in range(size):
-        value = a[k] + lower[k + 1, k]
-        alphas.append(value - lower[k, k - 1] if k else value)
-    betas = [None] + [pivots[k] / pivots[k - 1] for k in range(1, len(pivots))]
-    return alphas, betas
+class Lanczos:
+    def __init__(self, a):
+        self.a, self.lower, self.pivots, self.inverses = a, {}, [], []
+        self.alphas, self.betas = [], [None]
+
+    def row(self, k, entries, last=False):
+        reduced = []
+        for j in range(k):
+            value = entries[j]
+            for i in range(j):
+                value = value - reduced[i] * self.lower[j, i]
+            reduced.append(value)
+            self.lower[k, j] = value * self.inverses[j]
+        if k:
+            value = self.a[k - 1] + self.lower[k, k - 1]
+            self.alphas.append(value - self.lower[k - 1, k - 2] if k > 1 else value)
+        if last:
+            return
+        pivot = entries[k]
+        for i in range(k):
+            pivot = pivot - reduced[i] * self.lower[k, i]
+        if k:
+            self.betas.append(pivot * self.inverses[-1])
+        self.pivots.append(pivot)
+        self.inverses.append(1.0 / pivot)
 
 
 def added(x, y):
@@ -265,28 +265,28 @@
     def rolled(v, shift, axis):
         return pltpu.roll(v, shift % v.shape[axis], axis)
 
-    def strip_ready(src):
-        v = strip[src, 0]
-        strip_flow[...] = rolled(strip_coef[1, 0] * (v - rolled(v, -1, 1)), 1, 1)
-        strip_next[...] = rolled(strip[src, 1], -1, 1)
-
-    def tall_wide(c):
-        return c if isinstance(c, float) else jnp.concatenate([c] * (tall // SUB), axis=0)
-
-    def strip_step(src, prev, dst, a, b):
+    everywhere, inside = slice(0, tall), slice(GHOST, GHOST + R)
+
+    def strip_ready(src, t, lines):
+        v = strip[src, 0, lines, :]
+        strip_flow[t, lines, :] = rolled(strip_coef[1, 0, lines, :] * (v - rolled(v, -1, 1)), 1, 1)
+        strip_next[t, lines, :] = rolled(strip[src, 1, lines, :], -1, 1)
+
+    def strip_step(src, prev, dst, a, b, lines):
+        def spread(c):
+            return c if isinstance(c, float) else jnp.concatenate([c] * ((lines.stop - lines.start) // SUB), axis=0)
+
         for side in range(2):
-            v = strip[src, side]
-            flow = strip_coef[1, side] * (v - rolled(v, -1, 1))
-            fall = strip_coef[2, side] * (v - rolled(v, -1, 0))
-            value = (strip_coef[0, side] - tall_wide(a)) * v + (flow - rolled(flow, 1, 1)) + (fall - rolled(fall, 1, 0))
+            v = strip[src, side, lines, :]
+            flow = strip_coef[1, side, lines, :] * (v - rolled(v, -1, 1))
+            fall = strip_coef[2, side, lines, :] * (v - rolled(v, -1, 0))
+            value = (strip_coef[0, side, lines, :] - spread(a)) * v
+            value = value + (flow - rolled(flow, 1, 1)) + (fall - rolled(fall, 1, 0))
             if b is not None:
-                value = value - times(tall_wide(b), strip[prev, side])
-            strip[dst, side] = value
-
-    def step(src, prev, dst, a, b, reach):
-        first, count = D - reach, R + 2 * reach
-        unroll = next(u for u in (5, 6, 4, 3, 2, 1) if count % u == 0)
-
+                value = value - times(spread(b), strip[prev, side, lines, :])
+            strip[dst, side, lines, :] = value
+
+    def step(src, prev, dst, a, b, t, first, count, loop):
         def row(i, state):
             v, fall_above = state
             below = [basis[src, i + 1, j] for j in range(J)]
@@ -294,7 +294,7 @@
             line = pl.ds(i + (GHOST - D), 1)
             to_left = [rolled(v[j], -1, 1) for j in range(J)]
             beyond = jnp.where(
-                sub_id == SUB - 1, jnp.broadcast_to(strip_next[line, :], (SUB, LANES)), rolled(to_left[0], -1, 0)
+                sub_id == SUB - 1, jnp.broadcast_to(strip_next[t, line, :], (SUB, LANES)), rolled(to_left[0], -1, 0)
             )
             flow = [
                 coef[1, i, j] * (v[j] - jnp.where(lane_id == LANES - 1, to_left[j + 1] if j + 1 < J else beyond, to_left[j]))
@@ -302,7 +302,7 @@
             ]
             to_right = [rolled(f, 1, 1) for f in flow]
             before = jnp.where(
-                sub_id == 0, jnp.broadcast_to(strip_flow[line, :], (SUB, LANES)), rolled(to_right[J - 1], 1, 0)
+                sub_id == 0, jnp.broadcast_to(strip_flow[t, line, :], (SUB, LANES)), rolled(to_right[J - 1], 1, 0)
             )
             for j in range(J):
                 arriving = jnp.where(lane_id == 0, to_right[j - 1] if j else before, to_right[j])
@@ -312,20 +312,38 @@
                 basis[dst, i, j] = value
             return below, fall
 
+        v = [basis[src, first, j] for j in range(J)]
+        state = v, [coef[2, first - 1, j] * (basis[src, first - 1, j] - v[j]) for j in range(J)]
+        if not loop:
+            for i in range(first, first + count):
+                state = row(i, state)
+            return
+        unroll = next(u for u in (7, 6, 5, 4, 3, 2, 1) if count % u == 0)
+
         def body(n, state):
-            for t in range(unroll):
-                state = row(first + n * unroll + t, state)
+            for m in range(unroll):
+                state = row(first + n * unroll + m, state)
             return state
 
-        v = [basis[src, first, j] for j in range(J)]
-        fall = [coef[2, first - 1, j] * (basis[src, first - 1, j] - v[j]) for j in range(J)]
-        lax.fori_loop(0, count // unroll, body, (v, fall))
-
-    def advance(src, prev, dst, a, b, reach, more=True):
-        strip_ready(src)
-        step(src, prev, dst, a, b, reach)
-        if more:
-            strip_step(src, prev, dst, a, b)
+        lax.fori_loop(0, count // unroll, body, state)
+
+    def inner(recurrence, more, again):
+        lines = inside if again else everywhere
+        for t, (src, prev, dst, a, b) in enumerate(recurrence):
+            strip_ready(src, t, lines)
+            step(src, prev, dst, a, b, t, D + t + 1, R - 2 - 2 * t, True)
+            if more or t + 1 < len(recurrence):
+                strip_step(src, prev, dst, a, b, lines)
+
+    def outer(recurrence, more, again):
+        depth = len(recurrence)
+        for t, (src, prev, dst, a, b) in enumerate(recurrence):
+            if again:
+                strip_ready(src, t, everywhere)
+            step(src, prev, dst, a, b, t, D - (depth - 1 - t), depth, False)
+            step(src, prev, dst, a, b, t, D + R - 1 - t, depth, False)
+            if again and (more or t + 1 < depth):
+                strip_step(src, prev, dst, a, b, everywhere)
 
     def dots(pairs, base):
         for g in range(0, len(pairs), 8):
@@ -418,47 +436,55 @@
         copy(strip_coef.at[:, :, pl.ds(R, GHOST)], strip_coef.at[:, :, pl.ds(0, GHOST)], down, has_below, has_above),
     ]
     deeper = []
-    finish = None
     k = 0
     w_a = w_b = None
+    one = jnp.ones((SUB, LANES), jnp.float32)
     for n, block in enumerate(BLOCKS):
         slot = (lambda i: i) if k < SWITCH else w_slot
+        more = k + block < ITERS
         if n == 0:
-            arrive(opening + ghosts)
+            copies = opening + ghosts
         else:
-            first = send_rows(slot(k), 1, block) + send_rows(slot(k - 1), 2, block - 2)
+            copies = send_rows(slot(k), 1, block) + send_rows(slot(k - 1), 2, block - 2)
             if k == SWITCH:
-                first = first + send_strips([slot(k - 1), slot(k)])
+                copies = copies + send_strips([slot(k - 1), slot(k)])
             if n == 1 and BLOCKS[0] < D:
                 deeper = send_coefs(BLOCKS[0], D)
-            if k == KNOWN:
-                pairs = [(i, j) for i in range(KNOWN + 1) for j in range(i + 1)]
-                dots(pairs, 0)
-                finish = reduce(0, len(pairs))
-            if k == SWITCH:
-                combine([(w_slot(i), {s: weights[i][s] for s in range(i + 1)}) for i in range(1, SWITCH - 1)], D, R)
-                grams = [(i, j) for i in range(SWITCH + 1) for j in range(i + 1)]
-                dots([(w_slot(i), w_slot(j)) for i, j in grams], 0)
-            elif k > SWITCH:
-                more = [(i, j) for i in range(starts[n - 1] + 1, k + 1) for j in range(i + 1)]
-                dots([(w_slot(i), w_slot(j)) for i, j in more], len(grams))
-                grams = grams + more
-            arrive(first)
-            if block == D and deeper:
-                arrive(deeper)
-                deeper = []
-        for t in range(block):
-            a = v_a[k] if k < SWITCH else w_a[k]
-            b = v_b[k] if k < SWITCH else w_b[k]
-            advance(slot(k), slot(k - 1) if k else None, slot(k + 1), a, b, block - 1 - t, k + 1 < ITERS)
-            k += 1
+        v_or_w = (v_a, v_b) if k < SWITCH else (w_a, w_b)
+        recurrence = [
+            (slot(i), slot(i - 1) if i else None, slot(i + 1), v_or_w[0][i], v_or_w[1][i]) for i in range(k, k + block)
+        ]
+        if k == KNOWN:
+            pairs = [(i, j) for i in range(KNOWN + 1) for j in range(i + 1)]
+            dots(pairs, 0)
+            early = reduce(0, len(pairs))
         if k == SWITCH:
-            totals = finish()
-            gram = {pair: total for pair, total in zip(pairs, totals)}
-            alphas, betas = lanczos(gram, KNOWN, v_a)
-            w_a = alphas + [alphas[-1]] * (ITERS - KNOWN)
-            w_b = betas + [betas[-1]] * (ITERS - KNOWN)
-            one = jnp.ones((SUB, LANES), jnp.float32)
+            combine(final, D + D, R - 2 * D)
+        again = n == 0 or k == SWITCH
+        inner(recurrence, more, again)
+        if k == SWITCH:
+            combine([(w_slot(i), {s: weights[i][s] for s in range(i + 1)}) for i in range(1, SWITCH - 1)], D, R)
+            grams = [(i, j) for i in range(SWITCH + 1) for j in range(i + 1)]
+            dots([(w_slot(i), w_slot(j)) for i, j in grams], 0)
+        elif k > SWITCH:
+            added_pairs = [(i, j) for i in range(starts[n - 1] + 1, k + 1) for j in range(i + 1)]
+            dots([(w_slot(i), w_slot(j)) for i, j in added_pairs], len(grams))
+            grams = grams + added_pairs
+            if not more:
+                middle = reduce(1, len(grams))
+        arrive(copies)
+        if block == D and deeper:
+            arrive(deeper)
+            deeper = []
+        outer(recurrence, more, again)
+        k += block
+        if k == SWITCH:
+            entries = dict(zip(pairs, early()))
+            known = Lanczos(v_a)
+            for i in range(KNOWN + 1):
+                known.row(i, [entries[i, j] for j in range(i + 1)])
+            w_a = known.alphas + [known.alphas[-1]] * (ITERS - KNOWN)
+            w_b = known.betas + [known.betas[-1]] * (ITERS - KNOWN)
             weights = [[one]]
             for i in range(SWITCH):
                 value = applied(weights[i] + [None], v_a + [None], v_b + [None], i + 2)
@@ -467,9 +493,10 @@
                     value = [minus(p, times(w_b[i], q)) for p, q in zip(value, weights[i - 1] + [None] * 2)]
                 weights.append(value)
             final = [(w_slot(i), {s: weights[i][s] for s in range(i + 1)}) for i in (SWITCH - 1, SWITCH)]
-            combine(final, D, R)
             combine(final[:1], D - 1, 1)
             combine(final[:1], D + R, 1)
+            combine(final, D, D)
+            combine(final, D + R - D, D)
             for target, terms in final:
                 for side in range(2):
                     for band in range(bands):
@@ -479,28 +506,44 @@
                             total = added(total, times(weight, strip[s, side, own, :]))
                         strip[target, side, own, :] = total
 
-    more = [(i, j) for i in range(starts[-1] + 1, ITERS + 1) for j in range(i + 1) if j < ITERS]
-    dots([(w_slot(i), w_slot(j)) for i, j in more], len(grams))
-    grams = grams + more
-    totals = reduce(1, len(grams))()
-    gram = {pair: total for pair, total in zip(grams, totals)}
-    gram[ITERS, ITERS] = zero
-    alphas, betas = lanczos(gram, ITERS, w_a)
-    one = jnp.ones((SUB, LANES), jnp.float32)
+    full = starts[-1]
+    direct = [(i, j) for i in range(full + 1, ITERS + 1) for j in (i - 1, i) if j < ITERS]
+    dots([(w_slot(i), w_slot(j)) for i, j in direct], 0)
+    late = reduce(2, len(direct))
+    entries = dict(zip(grams, middle()))
+
+    def entry(i, j):
+        return entries[max(i, j), min(i, j)]
+
+    state = Lanczos(w_a)
     x, r, p = [None] * (ITERS + 1), [one], [one]
-    w_a = w_a + [None]
-    w_b = w_b + [None]
+    pad = [None]
     inverse = None
-    for i in range(ITERS):
-        pivot = alphas[i] if i == 0 else alphas[i] - betas[i] * inverse
+
+    def iterate(i):
+        nonlocal x, r, p, inverse
+        pivot = state.alphas[i] if i == 0 else state.alphas[i] - state.betas[i] * inverse
         inverse = 1.0 / pivot
-        image = applied(p + [None], w_a, w_b, i + 2)
+        image = applied(p + pad, w_a + pad, w_b + pad, i + 2)
         gain = SCALE * inverse
-        x = [added(q, times(gain, s)) for q, s in zip(x, p + [None] * (ITERS + 1 - len(p)))]
-        r = [minus(q, times(inverse, s)) for q, s in zip(r + [None], image)]
+        x = [added(q, times(gain, s)) for q, s in zip(x, p + pad * (ITERS + 1 - len(p)))]
+        r = [minus(q, times(inverse, s)) for q, s in zip(r + pad, image)]
         if i + 1 < ITERS:
-            ratio = betas[i + 1] * inverse * inverse
-            p = [added(q, times(ratio, s)) for q, s in zip(r, p + [None])]
+            ratio = state.betas[i + 1] * inverse * inverse
+            p = [added(q, times(ratio, s)) for q, s in zip(r, p + pad)]
+
+    for i in range(full + 1):
+        state.row(i, [entries[i, j] for j in range(i + 1)])
+        if i:
+            iterate(i - 1)
+    entries.update(zip(direct, late()))
+    for i in range(full + 1, ITERS + 1):
+        m = i - 1
+        for j in range(i - 1):
+            value = entry(m, j + 1) + (w_a[j] - w_a[m]) * entry(m, j) - w_b[m] * entry(m - 1, j)
+            entries[i, j] = value + w_b[j] * entry(m, j - 1) if j else value
+        state.row(i, [entries[i, j] for j in range(min(i + 1, ITERS))], i == ITERS)
+        iterate(m)
 
     def store(ref):
         def put(i, j, value):
@@ -550,14 +593,14 @@
                 held(3, high, chunk, SUB, LANES),
                 held(slots, 2, tall, LANES),
                 held(3, 2, tall, LANES),
-                held(tall, LANES),
-                held(tall, LANES),
+                held(DEPTH, tall, LANES),
+                held(DEPTH, tall, LANES),
                 held(2, bands, 4, SUB, LANES),
                 held(bands, 4, SUB, LANES),
                 held(bands, 4, SUB, LANES),
                 held(96, LANES),
-                held(2, nr * nc, 1, LANES),
-                dma((COPIES,)), dma((COPIES,)), dma((2, nr * nc)), dma((2, nr * nc)),
+                held(3, nr * nc, 1, LANES),
+                dma((COPIES,)), dma((COPIES,)), dma((3, nr * nc)), dma((3, nr * nc)),
             ],
             compiler_params=pltpu.CompilerParams(collective_id=0, has_side_effects=True),
         )(*(pieces(a) for a in inputs))

time: 54.1 us -> 47.5 us (0.88)
  Pallas kernels: 50.9 us -> 44.2 us
    pallas_call x1, Pallas kernels: 50.9 us -> 44.2 us  [on_device(): pl.pallas_call(functools.partial(kernel, nr, nc, rows, cols), out_shape=(...]
where the time goes in v1:
time: 47.5 us; the launch traced here: 47.3 us
  Pallas kernels  44.2 us (93%)
  local copies, waits for them, and re-layouts  2.42 us (5%)
  between operations  0.65 us (1%)
    pallas_call x1, Pallas kernels, on_device(): pl.pallas_call(functools.partial(kernel, nr, nc, rows, cols), out_shape=(...  44.2 us
    unnamed x4, local copies, waits for them, and re-layouts  2.42 us

profile of v1, /device:TPU:0, one launch (start us, length us, event | category | flops | bytes accessed | tf_op | source)
XLA Modules:
  0.0 47.3 jit_solution(13498024459248758573)
XLA Ops:
  0.6 44.2 %shard_map.68 = (f32[512,128]{1,0:T(8,128)}, f32[512,128]{1,0:T(8,128)}) custom-call(f32[512,128]{1,0:T(8,128)} %bitcast.35, s32[512,128]{1,0:T(8,128)} %bitcast.36, s32[512,128]{1,0:T(8,128)} %bitcast.37, f32[512,128]{1,0:T(8,128)} %bitcast.38, f32[512,128]{1,0:T(8,128)} %bitcast.39), custom_call_target="tpu_custom_call" | custom-call | tf_op jit(solution)/shard_map/pallas_call | solution.py:586
  44.9 0.0 copy-start
  44.9 1.7 %copy.9 = f32[16,4096]{1,0:T(8,128)} copy(f32[16,4096]{1,0:T(8,128)} %bitcast.41) | data formatting | bytes 524288
  46.6 0.0 copy-done
  46.6 0.7 %copy.10 = f32[16,4096]{1,0:T(8,128)} copy(f32[16,4096]{1,0:T(8,128)S(1)} %bitcast.40) | data formatting | bytes 524288
Async XLA Ops:
  44.9 1.7 %copy-start = (f32[512,128]{1,0:T(8,128)S(1)}, f32[512,128]{1,0:T(8,128)}, u32[]{:S(2)}) copy-start(f32[512,128]{1,0:T(8,128)} %get-tuple-element.5) | copy-start | bytes 786436

commit v2 on v1

--- a/solution.py
+++ b/solution.py
@@ -25,6 +25,7 @@
 DEPTH = max(BLOCKS)
 GHOST = SUB
 COPIES = 64
+MEETINGS = 16
 
 
 def each(start, stop, body):
@@ -89,11 +90,12 @@
 
 def kernel(
     nr, nc, rows, cols,
+    depth_in, mask_in, count_in, grad_h_in, grad_v_in,
+    x_out, r_out,
     depth, hit_mask, hit_count, grad_h, grad_v,
-    x_out, r_out,
     basis, coef, strip, strip_coef, strip_next, strip_flow,
     edge_send, edge_left, edge_right, folds, by_device,
-    send, recv, sum_send, sum_recv,
+    load, greet, send, recv, sum_send, sum_recv,
 ):
     me_r = lax.axis_index("rows")
     me_c = lax.axis_index("cols")
@@ -113,8 +115,46 @@
         other = lax.rem(me + k, devices)
         return (other // nc, lax.rem(other, nc))
 
+    def meet(semaphore, along_rows, along_cols):
+        ways = []
+        for far, others, me_there, there in (
+            (along_rows, nr, me_r, lambda k: (me_r + k, me_c)), (along_cols, nc, me_c, lambda k: (me_r, me_c + k)),
+        ):
+            if 0 < far < others:
+                ways += [(me_there >= far, there(-far)), (me_there < others - far, there(far))]
+        for exists, to in ways:
+            @pl.when(exists)
+            def _():
+                pl.semaphore_signal(semaphore, inc=1, device_id=to, device_id_type=MESH)
+        count = sum(exists.astype(jnp.int32) for exists, _ in ways)
+        return lambda: pl.semaphore_wait(semaphore, count)
+
     barrier = pltpu.get_barrier_semaphore()
-    each(1, devices, lambda k: pl.semaphore_signal(barrier, inc=1, device_id=peer(k), device_id_type=MESH))
+    greeted = meet(barrier, 1, 1)
+    loads = [
+        pltpu.make_async_copy(a, b, load.at[n])
+        for n, (a, b) in enumerate(
+            ((grad_h_in, grad_h), (grad_v_in, grad_v), (mask_in, hit_mask), (count_in, hit_count), (depth_in, depth))
+        )
+    ]
+    for c in loads:
+        c.start()
+
+    meetings = []
+    for axis, others in ((0, nr), (1, nc)):
+        far = 1
+        while far < others - 1 or (axis and far == 1 and others > 1):
+            meetings.append((far, 0) if axis == 0 else (0, far))
+            far *= 2
+    met = [0, None]
+
+    def meet_on():
+        if met[1] is not None:
+            met[1]()
+            met[1] = None
+        if met[0] < len(meetings):
+            met[1] = meet(greet.at[met[0]], *meetings[met[0]])
+            met[0] += 1
 
     sub_id = lax.broadcasted_iota(jnp.int32, (SUB, LANES), 0)
     lane_id = lax.broadcasted_iota(jnp.int32, (SUB, LANES), 1)
@@ -148,6 +188,8 @@
             s = jnp.where(jnp.logical_and(last_row, jnp.logical_not(has_below)), 0.0, s)
         return SCALE * confidence, e, s, confidence * read(depth)
 
+    for c in loads:
+        c.wait()
     for side in range(2):
         tile = (tiles - 1) * side
         for band in range(bands):
@@ -178,9 +220,13 @@
         for r in range(start, stop):
             row_coefficients(r, last and r == R - 1)
 
+    def inner_coefficients():
+        pairs = (R - 2 * D) // 2
+        lax.fori_loop(0, pairs, lambda i, c: ([row_coefficients(D + 2 * i + t, False) for t in range(2)], c)[1], 0)
+        coefficient_rows(D + 2 * pairs, R - D)
+
     coefficient_rows(0, D)
-    lax.fori_loop(0, (R - 2 * D) // 2, lambda i, c: ([row_coefficients(D + 2 * i + t, False) for t in range(2)], c)[1], 0)
-    coefficient_rows(D + (R - 2 * D) // 2 * 2, R, True)
+    coefficient_rows(R - D, R, True)
 
     def clear_ghost(first, strip_first):
         def _():
@@ -220,7 +266,7 @@
     def _():
         edge_right[...] = jnp.zeros_like(edge_right)
 
-    pl.semaphore_wait(barrier, devices - 1)
+    greeted()
 
     def send_rows(slot, first, count):
         if count <= 0:
@@ -424,7 +470,10 @@
         copy(edge_send.at[0], edge_right, lefthand, has_left, has_right),
         copy(edge_send.at[1], edge_left, righthand, has_right, has_left),
     ]
+    meet_on()
+    inner_coefficients()
     arrive(sides)
+    meet_on()
     for band in range(bands):
         own = slice(GHOST + band * SUB, GHOST + (band + 1) * SUB)
         for n in range(4):
@@ -457,11 +506,15 @@
         if k == KNOWN:
             pairs = [(i, j) for i in range(KNOWN + 1) for j in range(i + 1)]
             dots(pairs, 0)
+            while met[1] is not None:
+                meet_on()
             early = reduce(0, len(pairs))
         if k == SWITCH:
             combine(final, D + D, R - 2 * D)
         again = n == 0 or k == SWITCH
         inner(recurrence, more, again)
+        if k < KNOWN:
+            meet_on()
         if k == SWITCH:
             combine([(w_slot(i), {s: weights[i][s] for s in range(i + 1)}) for i in range(1, SWITCH - 1)], D, R)
             grams = [(i, j) for i in range(SWITCH + 1) for j in range(i + 1)]
@@ -470,10 +523,12 @@
             added_pairs = [(i, j) for i in range(starts[n - 1] + 1, k + 1) for j in range(i + 1)]
             dots([(w_slot(i), w_slot(j)) for i, j in added_pairs], len(grams))
             grams = grams + added_pairs
-            if not more:
-                middle = reduce(1, len(grams))
+        if not more:
+            middle = reduce(1, len(grams))
         arrive(copies)
-        if block == D and deeper:
+        if k < KNOWN:
+            meet_on()
+        if block > BLOCKS[0] and deeper:
             arrive(deeper)
             deeper = []
         outer(recurrence, more, again)
@@ -586,9 +641,10 @@
         x, r = pl.pallas_call(
             functools.partial(kernel, nr, nc, rows, cols),
             out_shape=(block, block),
-            in_specs=[pl.BlockSpec(memory_space=pltpu.VMEM)] * 5,
+            in_specs=[pl.BlockSpec(memory_space=pl.ANY)] * 5,
             out_specs=[pl.BlockSpec(memory_space=pltpu.VMEM)] * 2,
-            scratch_shapes=[
+            scratch_shapes=[pltpu.VMEM(block.shape, a.dtype) for a in inputs]
+            + [
                 held(slots, high, chunk, SUB, LANES),
                 held(3, high, chunk, SUB, LANES),
                 held(slots, 2, tall, LANES),
@@ -600,6 +656,7 @@
                 held(bands, 4, SUB, LANES),
                 held(96, LANES),
                 held(3, nr * nc, 1, LANES),
+                dma((5,)), pltpu.SemaphoreType.REGULAR((MEETINGS,)),
                 dma((COPIES,)), dma((COPIES,)), dma((3, nr * nc)), dma((3, nr * nc)),
             ],
             compiler_params=pltpu.CompilerParams(collective_id=0, has_side_effects=True),

time: 47.5 us -> 44.5 us (0.937)
  Pallas kernels: 44.2 us -> 41.3 us
    pallas_call x1, Pallas kernels: 44.2 us -> 41.3 us  [on_device(): pl.pallas_call(functools.partial(kernel, nr, nc, rows, cols), out_shape=(...]
where the time goes in v2:
time: 44.5 us; the launch traced here: 44.3 us
  Pallas kernels  41.3 us (93%)
  local copies, waits for them, and re-layouts  2.42 us (5%)
  between operations  0.65 us (1%)
    pallas_call x1, Pallas kernels, on_device(): pl.pallas_call(functools.partial(kernel, nr, nc, rows, cols), out_shape=(...  41.3 us
    unnamed x4, local copies, waits for them, and re-layouts  2.42 us

profile of v2, /device:TPU:0, one launch (start us, length us, event | category | flops | bytes accessed | tf_op | source)
XLA Modules:
  0.0 44.3 jit_solution(4289008267098362310)
XLA Ops:
  0.6 41.3 %shard_map.68 = (f32[512,128]{1,0:T(8,128)}, f32[512,128]{1,0:T(8,128)}) custom-call(f32[512,128]{1,0:T(8,128)} %bitcast.35, s32[512,128]{1,0:T(8,128)} %bitcast.36, s32[512,128]{1,0:T(8,128)} %bitcast.37, f32[512,128]{1,0:T(8,128)} %bitcast.38, f32[512,128]{1,0:T(8,128)} %bitcast.39), custom_call_target="tpu_custom_call" | custom-call | tf_op jit(solution)/shard_map/pallas_call | solution.py:641
  41.9 0.0 copy-start
  41.9 1.7 %copy.9 = f32[16,4096]{1,0:T(8,128)} copy(f32[16,4096]{1,0:T(8,128)} %bitcast.41) | data formatting | bytes 524288
  43.6 0.0 copy-done
  43.6 0.7 %copy.10 = f32[16,4096]{1,0:T(8,128)} copy(f32[16,4096]{1,0:T(8,128)S(1)} %bitcast.40) | data formatting | bytes 524288
Async XLA Ops:
  41.9 1.7 %copy-start = (f32[512,128]{1,0:T(8,128)S(1)}, f32[512,128]{1,0:T(8,128)}, u32[]{:S(2)}) copy-start(f32[512,128]{1,0:T(8,128)} %get-tuple-element.5) | copy-start | bytes 786436

commit v3 on v2

--- a/solution.py
+++ b/solution.py
@@ -73,6 +73,23 @@
 
 def minus(x, y):
     return x if y is None else (-y if x is None else x - y)
+
+
+def chained(full, stop):
+    return [(i, j) for i in range(full + 1, stop + 1) for j in (i - 1, i)]
+
+
+def fill(entries, i, a, b):
+    m = i - 1
+
+    def entry(p, q):
+        return entries[max(p, q), min(p, q)]
+
+    for j in range(m):
+        value = entry(m, j + 1) - times(b[m], entry(m - 1, j))
+        if not (isinstance(a[j], float) and a[j] == a[m]):
+            value = value + (a[j] - a[m]) * entry(m, j)
+        entries[i, j] = value + times(b[j], entry(m, j - 1)) if j else value
 
 
 def applied(p, a, b, size):
@@ -161,7 +178,7 @@
     zero = jnp.zeros((SUB, LANES), jnp.float32)
 
     used = [0]
-    pending = []
+    pending, reductions = [], []
 
     def copy(src, dst, to, sends, receives):
         k = used[0]
@@ -236,11 +253,10 @@
                         coef[n, first + t, j] = zero
                     for slot in exchanged:
                         basis[slot, first + t, j] = zero
-            for side in range(2):
-                for n in range(3):
-                    strip_coef[n, side, strip_first : strip_first + GHOST, :] = zero
-                for slot in strips_exchanged:
-                    strip[slot, side, strip_first : strip_first + GHOST, :] = zero
+            for n in range(3):
+                strip_coef[n, strip_first : strip_first + GHOST, :] = zero
+            for slot in strips_exchanged:
+                strip[slot, strip_first : strip_first + GHOST, :] = zero
 
         return _
 
@@ -299,12 +315,12 @@
         for slot in slots:
             copies.append(
                 copy(
-                    strip.at[slot, :, pl.ds(GHOST, GHOST)], strip.at[slot, :, pl.ds(GHOST + R, GHOST)],
+                    strip.at[slot, pl.ds(GHOST, GHOST)], strip.at[slot, pl.ds(GHOST + R, GHOST)],
                     up, has_above, has_below,
                 )
             )
             copies.append(
-                copy(strip.at[slot, :, pl.ds(R, GHOST)], strip.at[slot, :, pl.ds(0, GHOST)], down, has_below, has_above)
+                copy(strip.at[slot, pl.ds(R, GHOST)], strip.at[slot, pl.ds(0, GHOST)], down, has_below, has_above)
             )
         return copies
 
@@ -314,23 +330,22 @@
     everywhere, inside = slice(0, tall), slice(GHOST, GHOST + R)
 
     def strip_ready(src, t, lines):
-        v = strip[src, 0, lines, :]
-        strip_flow[t, lines, :] = rolled(strip_coef[1, 0, lines, :] * (v - rolled(v, -1, 1)), 1, 1)
-        strip_next[t, lines, :] = rolled(strip[src, 1, lines, :], -1, 1)
+        v = strip[src, lines, :]
+        strip_flow[t, lines, :] = rolled(strip_coef[1, lines, :] * (v - rolled(v, -1, 1)), 1, 1)
+        strip_next[t, lines, :] = rolled(v, HALF - 1, 1)
 
     def strip_step(src, prev, dst, a, b, lines):
         def spread(c):
             return c if isinstance(c, float) else jnp.concatenate([c] * ((lines.stop - lines.start) // SUB), axis=0)
 
-        for side in range(2):
-            v = strip[src, side, lines, :]
-            flow = strip_coef[1, side, lines, :] * (v - rolled(v, -1, 1))
-            fall = strip_coef[2, side, lines, :] * (v - rolled(v, -1, 0))
-            value = (strip_coef[0, side, lines, :] - spread(a)) * v
-            value = value + (flow - rolled(flow, 1, 1)) + (fall - rolled(fall, 1, 0))
-            if b is not None:
-                value = value - times(spread(b), strip[prev, side, lines, :])
-            strip[dst, side, lines, :] = value
+        v = strip[src, lines, :]
+        flow = strip_coef[1, lines, :] * (v - rolled(v, -1, 1))
+        fall = strip_coef[2, lines, :] * (v - rolled(v, -1, 0))
+        value = (strip_coef[0, lines, :] - spread(a)) * v
+        value = value + (flow - rolled(flow, 1, 1)) + (fall - rolled(fall, 1, 0))
+        if b is not None:
+            value = value - times(spread(b), strip[prev, lines, :])
+        strip[dst, lines, :] = value
 
     def step(src, prev, dst, a, b, t, first, count, loop):
         def row(i, state):
@@ -439,6 +454,7 @@
             )
 
         each(1, devices, lambda k: outgoing(k).start())
+        reductions.append(outgoing)
 
         def finish():
             def arrival(k):
@@ -450,7 +466,6 @@
                 ).wait_recv()
 
             each(1, devices, arrival)
-            each(1, devices, lambda k: outgoing(k).wait_send())
             if devices <= 32:
                 parts = [by_device[slot, k] for k in range(devices)]
                 while len(parts) > 1:
@@ -477,12 +492,14 @@
     for band in range(bands):
         own = slice(GHOST + band * SUB, GHOST + (band + 1) * SUB)
         for n in range(4):
+            left_border = jnp.where(lane_id < HALF, edge_send[0, band, n], edge_left[band, n])
+            right_border = jnp.where(lane_id < HALF, edge_right[band, n], edge_send[1, band, n])
             here = strip_coef.at[n] if n < 3 else strip.at[0]
-            here[0, own, :] = jnp.where(lane_id < HALF, edge_send[0, band, n], edge_left[band, n])
-            here[1, own, :] = jnp.where(lane_id < HALF, edge_right[band, n], edge_send[1, band, n])
+            at_left = jnp.logical_or(lane_id < HALF // 2, lane_id >= LANES - HALF // 2)
+            here[own, :] = jnp.where(at_left, left_border, rolled(right_border, HALF, 1))
     ghosts = send_strips([0]) + [
-        copy(strip_coef.at[:, :, pl.ds(GHOST, GHOST)], strip_coef.at[:, :, pl.ds(GHOST + R, GHOST)], up, has_above, has_below),
-        copy(strip_coef.at[:, :, pl.ds(R, GHOST)], strip_coef.at[:, :, pl.ds(0, GHOST)], down, has_below, has_above),
+        copy(strip_coef.at[:, pl.ds(GHOST, GHOST)], strip_coef.at[:, pl.ds(GHOST + R, GHOST)], up, has_above, has_below),
+        copy(strip_coef.at[:, pl.ds(R, GHOST)], strip_coef.at[:, pl.ds(0, GHOST)], down, has_below, has_above),
     ]
     deeper = []
     k = 0
@@ -491,6 +508,14 @@
     for n, block in enumerate(BLOCKS):
         slot = (lambda i: i) if k < SWITCH else w_slot
         more = k + block < ITERS
+        if k == KNOWN:
+            while met[1] is not None:
+                meet_on()
+            base = starts[n - 1]
+            direct = chained(base, KNOWN)
+            dots(direct, len(pairs))
+            pairs = pairs + direct
+            early = reduce(0, len(pairs))
         if n == 0:
             copies = opening + ghosts
         else:
@@ -503,12 +528,6 @@
         recurrence = [
             (slot(i), slot(i - 1) if i else None, slot(i + 1), v_or_w[0][i], v_or_w[1][i]) for i in range(k, k + block)
         ]
-        if k == KNOWN:
-            pairs = [(i, j) for i in range(KNOWN + 1) for j in range(i + 1)]
-            dots(pairs, 0)
-            while met[1] is not None:
-                meet_on()
-            early = reduce(0, len(pairs))
         if k == SWITCH:
             combine(final, D + D, R - 2 * D)
         again = n == 0 or k == SWITCH
@@ -525,6 +544,9 @@
             grams = grams + added_pairs
         if not more:
             middle = reduce(1, len(grams))
+        if k + block == KNOWN:
+            pairs = [(i, j) for i in range(k + 1) for j in range(i + 1)]
+            dots(pairs, 0)
         arrive(copies)
         if k < KNOWN:
             meet_on()
@@ -536,6 +558,8 @@
         if k == SWITCH:
             entries = dict(zip(pairs, early()))
             known = Lanczos(v_a)
+            for i in range(base + 1, KNOWN + 1):
+                fill(entries, i, v_a, v_b)
             for i in range(KNOWN + 1):
                 known.row(i, [entries[i, j] for j in range(i + 1)])
             w_a = known.alphas + [known.alphas[-1]] * (ITERS - KNOWN)
@@ -553,22 +577,18 @@
             combine(final, D, D)
             combine(final, D + R - D, D)
             for target, terms in final:
-                for side in range(2):
-                    for band in range(bands):
-                        own = slice(GHOST + band * SUB, GHOST + (band + 1) * SUB)
-                        total = None
-                        for s, weight in terms.items():
-                            total = added(total, times(weight, strip[s, side, own, :]))
-                        strip[target, side, own, :] = total
+                for band in range(bands):
+                    own = slice(GHOST + band * SUB, GHOST + (band + 1) * SUB)
+                    total = None
+                    for s, weight in terms.items():
+                        total = added(total, times(weight, strip[s, own, :]))
+                    strip[target, own, :] = total
 
     full = starts[-1]
-    direct = [(i, j) for i in range(full + 1, ITERS + 1) for j in (i - 1, i) if j < ITERS]
+    direct = chained(full, ITERS)[:-1]
     dots([(w_slot(i), w_slot(j)) for i, j in direct], 0)
     late = reduce(2, len(direct))
     entries = dict(zip(grams, middle()))
-
-    def entry(i, j):
-        return entries[max(i, j), min(i, j)]
 
     state = Lanczos(w_a)
     x, r, p = [None] * (ITERS + 1), [one], [one]
@@ -593,12 +613,9 @@
             iterate(i - 1)
     entries.update(zip(direct, late()))
     for i in range(full + 1, ITERS + 1):
-        m = i - 1
-        for j in range(i - 1):
-            value = entry(m, j + 1) + (w_a[j] - w_a[m]) * entry(m, j) - w_b[m] * entry(m - 1, j)
-            entries[i, j] = value + w_b[j] * entry(m, j - 1) if j else value
+        fill(entries, i, w_a, w_b)
         state.row(i, [entries[i, j] for j in range(min(i + 1, ITERS))], i == ITERS)
-        iterate(m)
+        iterate(i - 1)
 
     def store(ref):
         def put(i, j, value):
@@ -616,6 +633,8 @@
     )
     for c, sends in pending:
         pl.when(sends)(c.wait_send)
+    for outgoing in reductions:
+        each(1, devices, lambda k: outgoing(k).wait_send())
 
 
 def solution(mesh):
@@ -640,15 +659,15 @@
         dma = pltpu.SemaphoreType.DMA
         x, r = pl.pallas_call(
             functools.partial(kernel, nr, nc, rows, cols),
-            out_shape=(block, block),
+            out_shape=(pltpu.VMEM(block.shape, jnp.float32),) * 2,
             in_specs=[pl.BlockSpec(memory_space=pl.ANY)] * 5,
             out_specs=[pl.BlockSpec(memory_space=pltpu.VMEM)] * 2,
             scratch_shapes=[pltpu.VMEM(block.shape, a.dtype) for a in inputs]
             + [
                 held(slots, high, chunk, SUB, LANES),
                 held(3, high, chunk, SUB, LANES),
-                held(slots, 2, tall, LANES),
-                held(3, 2, tall, LANES),
+                held(slots, tall, LANES),
+                held(3, tall, LANES),
                 held(DEPTH, tall, LANES),
                 held(DEPTH, tall, LANES),
                 held(2, bands, 4, SUB, LANES),

time: 44.5 us -> 40.9 us (0.919)
  Pallas kernels: 41.3 us -> 38.7 us
  local copies, waits for them, and re-layouts: 2.42 us -> 1.41 us
    pallas_call x1, Pallas kernels: 41.3 us -> 38.7 us  [on_device(): pl.pallas_call(functools.partial(kernel, nr, nc, rows, cols), out_shape=(...]
    unnamed x4 -> x2, local copies, waits for them, and re-layouts: 2.42 us -> 1.41 us
where the time goes in v3:
time: 40.9 us; the launch traced here: 40.8 us
  Pallas kernels  38.7 us (95%)
  local copies, waits for them, and re-layouts  1.41 us (3%)
  between operations  0.64 us (2%)
    pallas_call x1, Pallas kernels, on_device(): pl.pallas_call(functools.partial(kernel, nr, nc, rows, cols), out_shape=(...  38.7 us
    unnamed x2, local copies, waits for them, and re-layouts  1.41 us

profile of v3, /device:TPU:0, one launch (start us, length us, event | category | flops | bytes accessed | tf_op | source)
XLA Modules:
  0.0 40.8 jit_solution(12795296027880064632)
XLA Ops:
  0.6 38.7 %shard_map.68 = (f32[512,128]{1,0:T(8,128)S(1)}, f32[512,128]{1,0:T(8,128)S(1)}) custom-call(f32[512,128]{1,0:T(8,128)} %bitcast.37, s32[512,128]{1,0:T(8,128)} %bitcast.38, s32[512,128]{1,0:T(8,128)} %bitcast.39, f32[512,128]{1,0:T(8,128)} %bitcast.40, f32[512,128]{1,0:T(8,128)} %bitcast.41), custom_call_target="tpu_custom_call" | custom-call | tf_op jit(solution)/shard_map/pallas_call | solution.py:660
  39.4 0.7 %copy.9 = f32[16,4096]{1,0:T(8,128)} copy(f32[16,4096]{1,0:T(8,128)S(1)} %bitcast.36) | data formatting | bytes 524288
  40.1 0.7 %copy.10 = f32[16,4096]{1,0:T(8,128)} copy(f32[16,4096]{1,0:T(8,128)S(1)} %bitcast.35) | data formatting | bytes 524288

commit v4 on v3

--- a/solution.py
+++ b/solution.py
@@ -86,10 +86,10 @@
         return entries[max(p, q), min(p, q)]
 
     for j in range(m):
-        value = entry(m, j + 1) - times(b[m], entry(m - 1, j))
+        value = minus(entry(m, j + 1), times(b[m], entry(m - 1, j)))
         if not (isinstance(a[j], float) and a[j] == a[m]):
             value = value + (a[j] - a[m]) * entry(m, j)
-        entries[i, j] = value + times(b[j], entry(m, j - 1)) if j else value
+        entries[i, j] = added(value, times(b[j], entry(m, j - 1))) if j else value
 
 
 def applied(p, a, b, size):
@@ -270,7 +270,7 @@
         | {(k - 1 if k < SWITCH else w_slot(k - 1)) for k in starts if k > 0}
         | set(range(SWITCH))
     )
-    strips_exchanged = [0, w_slot(SWITCH - 1), w_slot(SWITCH)]
+    strips_exchanged = [0, w_slot(SWITCH)]
     pl.when(jnp.logical_not(has_above))(clear_ghost(0, 0))
     pl.when(jnp.logical_not(has_below))(clear_ghost(D + R, GHOST + R))
 
@@ -479,6 +479,7 @@
 
     v_a = [CENTER] * SWITCH
     v_b = [None, 2.0 * SPREAD] + [SPREAD] * (SWITCH - 1)
+    v_b[KNOWN] = None
 
     opening = send_rows(0, 1, BLOCKS[0]) + send_coefs(0, BLOCKS[0])
     sides = [
@@ -519,9 +520,11 @@
         if n == 0:
             copies = opening + ghosts
         else:
-            copies = send_rows(slot(k), 1, block) + send_rows(slot(k - 1), 2, block - 2)
+            copies = send_rows(slot(k), 1, block)
             if k == SWITCH:
-                copies = copies + send_strips([slot(k - 1), slot(k)])
+                copies = copies + send_strips([slot(k)])
+            elif k != KNOWN:
+                copies = copies + send_rows(slot(k - 1), 2, block - 2)
             if n == 1 and BLOCKS[0] < D:
                 deeper = send_coefs(BLOCKS[0], D)
         v_or_w = (v_a, v_b) if k < SWITCH else (w_a, w_b)
@@ -535,11 +538,11 @@
         if k < KNOWN:
             meet_on()
         if k == SWITCH:
-            combine([(w_slot(i), {s: weights[i][s] for s in range(i + 1)}) for i in range(1, SWITCH - 1)], D, R)
+            combine([(w_slot(i), {s: weights[i][s] for s in range(i + 1)}) for i in range(1, SWITCH)], D, R)
             grams = [(i, j) for i in range(SWITCH + 1) for j in range(i + 1)]
             dots([(w_slot(i), w_slot(j)) for i, j in grams], 0)
         elif k > SWITCH:
-            added_pairs = [(i, j) for i in range(starts[n - 1] + 1, k + 1) for j in range(i + 1)]
+            added_pairs = chained(starts[n - 1], k)
             dots([(w_slot(i), w_slot(j)) for i, j in added_pairs], len(grams))
             grams = grams + added_pairs
         if not more:
@@ -571,9 +574,8 @@
                 if i:
                     value = [minus(p, times(w_b[i], q)) for p, q in zip(value, weights[i - 1] + [None] * 2)]
                 weights.append(value)
-            final = [(w_slot(i), {s: weights[i][s] for s in range(i + 1)}) for i in (SWITCH - 1, SWITCH)]
-            combine(final[:1], D - 1, 1)
-            combine(final[:1], D + R, 1)
+            w_b[SWITCH] = None
+            final = [(w_slot(SWITCH), dict(enumerate(weights[SWITCH])))]
             combine(final, D, D)
             combine(final, D + R - D, D)
             for target, terms in final:
@@ -608,6 +610,8 @@
             p = [added(q, times(ratio, s)) for q, s in zip(r, p + pad)]
 
     for i in range(full + 1):
+        if i > SWITCH:
+            fill(entries, i, w_a, w_b)
         state.row(i, [entries[i, j] for j in range(i + 1)])
         if i:
             iterate(i - 1)

time: 40.9 us -> 40.1 us (0.980)
  Pallas kernels: 38.7 us -> 37.9 us
    pallas_call x1, Pallas kernels: 38.7 us -> 37.9 us  [on_device(): pl.pallas_call(functools.partial(kernel, nr, nc, rows, cols), out_shape=(...]
where the time goes in v4:
time: 40.1 us; the launch traced here: 39.9 us
  Pallas kernels  37.9 us (95%)
  local copies, waits for them, and re-layouts  1.41 us (4%)
  between operations  0.64 us (2%)
    pallas_call x1, Pallas kernels, on_device(): pl.pallas_call(functools.partial(kernel, nr, nc, rows, cols), out_shape=(...  37.9 us
    unnamed x2, local copies, waits for them, and re-layouts  1.41 us

profile of v4, /device:TPU:0, one launch (start us, length us, event | category | flops | bytes accessed | tf_op | source)
XLA Modules:
  0.0 39.9 jit_solution(2851691373514673219)
XLA Ops:
  0.6 37.9 %shard_map.68 = (f32[512,128]{1,0:T(8,128)S(1)}, f32[512,128]{1,0:T(8,128)S(1)}) custom-call(f32[512,128]{1,0:T(8,128)} %bitcast.37, s32[512,128]{1,0:T(8,128)} %bitcast.38, s32[512,128]{1,0:T(8,128)} %bitcast.39, f32[512,128]{1,0:T(8,128)} %bitcast.40, f32[512,128]{1,0:T(8,128)} %bitcast.41), custom_call_target="tpu_custom_call" | custom-call | tf_op jit(solution)/shard_map/pallas_call | solution.py:664
  38.5 0.7 %copy.9 = f32[16,4096]{1,0:T(8,128)} copy(f32[16,4096]{1,0:T(8,128)S(1)} %bitcast.36) | data formatting | bytes 524288
  39.2 0.7 %copy.10 = f32[16,4096]{1,0:T(8,128)} copy(f32[16,4096]{1,0:T(8,128)S(1)} %bitcast.35) | data formatting | bytes 524288

commit v5 on v4

--- a/solution.py
+++ b/solution.py
@@ -108,12 +108,13 @@
 def kernel(
     nr, nc, rows, cols,
     depth_in, mask_in, count_in, grad_h_in, grad_v_in,
-    x_out, r_out,
+    both_out,
     depth, hit_mask, hit_count, grad_h, grad_v,
     basis, coef, strip, strip_coef, strip_next, strip_flow,
     edge_send, edge_left, edge_right, folds, by_device,
     load, greet, send, recv, sum_send, sum_recv,
 ):
+    x_out, r_out = both_out.at[0], both_out.at[1]
     me_r = lax.axis_index("rows")
     me_c = lax.axis_index("cols")
     J = cols // (SUB * LANES)
@@ -661,11 +662,11 @@
         high, tall = rows + 2 * DEPTH, rows + 2 * GHOST
         slots = SWITCH + ITERS + 1
         dma = pltpu.SemaphoreType.DMA
-        x, r = pl.pallas_call(
+        both = pl.pallas_call(
             functools.partial(kernel, nr, nc, rows, cols),
-            out_shape=(pltpu.VMEM(block.shape, jnp.float32),) * 2,
+            out_shape=pltpu.VMEM((2,) + block.shape, jnp.float32),
             in_specs=[pl.BlockSpec(memory_space=pl.ANY)] * 5,
-            out_specs=[pl.BlockSpec(memory_space=pltpu.VMEM)] * 2,
+            out_specs=pl.BlockSpec(memory_space=pltpu.VMEM),
             scratch_shapes=[pltpu.VMEM(block.shape, a.dtype) for a in inputs]
             + [
                 held(slots, high, chunk, SUB, LANES),
@@ -684,7 +685,7 @@
             ],
             compiler_params=pltpu.CompilerParams(collective_id=0, has_side_effects=True),
         )(*(pieces(a) for a in inputs))
-        return whole(x), whole(r)
+        return whole(both[0]), whole(both[1])
 
     spec = P("rows", "cols")
     return jax.shard_map(

time: 40.1 us -> 39.5 us (0.985)
  local copies, waits for them, and re-layouts: 1.41 us -> 0.82 us
    unnamed x2 -> x0, local copies, waits for them, and re-layouts: 1.41 us -> none
    slice x0 -> x1, local copies, waits for them, and re-layouts: none -> 0.82 us  [on_device(): return (whole(both[0]), whole(both[1]))]
where the time goes in v5:
time: 39.5 us; the launch traced here: 39.4 us
  Pallas kernels  37.9 us (96%)
  local copies, waits for them, and re-layouts  0.82 us (2%)
  between operations  0.64 us (2%)
    pallas_call x1, Pallas kernels, on_device(): pl.pallas_call(functools.partial(kernel, nr, nc, rows, cols), out_shape=p...  37.9 us
    slice x1, local copies, waits for them, and re-layouts, on_device(): return (whole(both[0]), whole(both[1]))  0.82 us

profile of v5, /device:TPU:0, one launch (start us, length us, event | category | flops | bytes accessed | tf_op | source)
XLA Modules:
  0.0 39.4 jit_solution(8311441746085653684)
XLA Ops:
  0.6 37.9 %shard_map.68 = f32[2,512,128]{2,1,0:T(8,128)S(1)} custom-call(f32[512,128]{1,0:T(8,128)} %bitcast.35, s32[512,128]{1,0:T(8,128)} %bitcast.36, s32[512,128]{1,0:T(8,128)} %bitcast.37, f32[512,128]{1,0:T(8,128)} %bitcast.38, f32[512,128]{1,0:T(8,128)} %bitcast.39), custom_call_target="tpu_custom_call" | custom-call | tf_op jit(solution)/shard_map/pallas_call | solution.py:665
  38.5 0.8 %fusion = (f32[1,512,128]{2,1,0:T(8,128)}, f32[1,512,128]{2,1,0:T(8,128)}) fusion(f32[2,512,128]{2,1,0:T(8,128)S(1)} %shard_map.68), kind=kLoop, calls=%fused_computation | loop fusion | bytes 1048576 | tf_op jit(solution)/shard_map/slice | solution.py:688

commit v6 on v5

--- a/solution.py
+++ b/solution.py
@@ -19,9 +19,9 @@
 SCALE = 0.25
 CENTER = 9.0 * SCALE
 SPREAD = 16.0 * SCALE * SCALE
-BLOCKS = (2, 2, 3, 3, 2)
+BLOCKS = (2, 2, 4, 4)
 KNOWN = 4
-SWITCH = 7
+SWITCH = 8
 DEPTH = max(BLOCKS)
 GHOST = SUB
 COPIES = 64

time: 39.5 us -> 39.5 us (level)
  no operation moved by 1% of the time
where the time goes in v6:
time: 39.5 us; the launch traced here: 39.4 us
  Pallas kernels  37.9 us (96%)
  local copies, waits for them, and re-layouts  0.82 us (2%)
  between operations  0.64 us (2%)
    pallas_call x1, Pallas kernels, on_device(): pl.pallas_call(functools.partial(kernel, nr, nc, rows, cols), out_shape=p...  37.9 us
    slice x1, local copies, waits for them, and re-layouts, on_device(): return (whole(both[0]), whole(both[1]))  0.82 us

profile of v6, /device:TPU:0, one launch (start us, length us, event | category | flops | bytes accessed | tf_op | source)
XLA Modules:
  0.0 39.4 jit_solution(8729432079121203851)
XLA Ops:
  0.6 37.9 %shard_map.68 = f32[2,512,128]{2,1,0:T(8,128)S(1)} custom-call(f32[512,128]{1,0:T(8,128)} %bitcast.35, s32[512,128]{1,0:T(8,128)} %bitcast.36, s32[512,128]{1,0:T(8,128)} %bitcast.37, f32[512,128]{1,0:T(8,128)} %bitcast.38, f32[512,128]{1,0:T(8,128)} %bitcast.39), custom_call_target="tpu_custom_call" | custom-call | tf_op jit(solution)/shard_map/pallas_call | solution.py:665
  38.6 0.8 %fusion = (f32[1,512,128]{2,1,0:T(8,128)}, f32[1,512,128]{2,1,0:T(8,128)}) fusion(f32[2,512,128]{2,1,0:T(8,128)S(1)} %shard_map.68), kind=kLoop, calls=%fused_computation | loop fusion | bytes 1048576 | tf_op jit(solution)/shard_map/slice | solution.py:688
